TPU v7x, 32 devices: a whole 2x2x4 slice. The times are simulated.
32 devices in a mesh: wide: 8 (over z, y), narrow: 4 (over x, core).
Axes of the slice: x: 2, y: 2, z: 4, core: 2. Of those that a mesh axis runs over, the one named last changes fastest.
Arguments:
- patches: bfloat16 [128, 256, 768], P(('wide', 'narrow')), may hold values from -6 to 6
- counts: int32 [128], P(('wide', 'narrow')), may hold values from 16 to 256, as said below
- cotangent: bfloat16 [128, 256, 768], P(('wide', 'narrow')), may hold values from -6 to 6
- input_weight: bfloat16 [768, 2304], P(('wide', 'narrow')), may hold values from -0.21875 to 0.21875
- output_weight: bfloat16 [768, 768], P(('wide', 'narrow')), may hold values from -0.875 to 0.875
- expand_weight: bfloat16 [768, 3072], P(('wide', 'narrow')), may hold values from -0.21875 to 0.21875
- reduce_weight: bfloat16 [3072, 768], P(('wide', 'narrow')), may hold values from -0.15625 to 0.15625
- norm1_gain: bfloat16 [768], P(('wide', 'narrow')), may hold values from 0.5 to 1.5
- norm1_shift: bfloat16 [768], P(('wide', 'narrow')), may hold values from -1.75 to 1.75
- query_bias: bfloat16 [768], P(('wide', 'narrow')), may hold values from -3 to 3
- value_bias: bfloat16 [768], P(('wide', 'narrow')), may hold values from -1.75 to 1.75
- output_bias: bfloat16 [768], P(('wide', 'narrow')), may hold values from -1.75 to 1.75
- branch1_scale: bfloat16 [768], P(('wide', 'narrow')), may hold values from 0.29882812 to 1.5
- norm2_gain: bfloat16 [768], P(('wide', 'narrow')), may hold values from 0.5 to 1.5
- norm2_shift: bfloat16 [768], P(('wide', 'narrow')), may hold values from -1.75 to 1.75
- expand_bias: bfloat16 [3072], P(('wide', 'narrow')), may hold values from -3 to 3
- reduce_bias: bfloat16 [768], P(('wide', 'narrow')), may hold values from -1.75 to 1.75
- branch2_scale: bfloat16 [768], P(('wide', 'narrow')), may hold values from 0.29882812 to 1.5
Outputs:
- activations: bfloat16 [128, 256, 768], P(('wide', 'narrow'))
- input_grad: float32 [128, 256, 768], P(('wide', 'narrow'))
- input_weight_grad: float32 [768, 2304], P(('wide', 'narrow'))
- output_weight_grad: float32 [768, 768], P(('wide', 'narrow'))
- expand_weight_grad: float32 [768, 3072], P(('wide', 'narrow'))
- reduce_weight_grad: float32 [3072, 768], P(('wide', 'narrow'))
- norm1_gain_grad: float32 [768], P(('wide', 'narrow'))
- norm1_shift_grad: float32 [768], P(('wide', 'narrow'))
- query_bias_grad: float32 [768], P(('wide', 'narrow'))
- value_bias_grad: float32 [768], P(('wide', 'narrow'))
- output_bias_grad: float32 [768], P(('wide', 'narrow'))
- branch1_scale_grad: float32 [768], P(('wide', 'narrow'))
- norm2_gain_grad: float32 [768], P(('wide', 'narrow'))
- norm2_shift_grad: float32 [768], P(('wide', 'narrow'))
- expand_bias_grad: float32 [3072], P(('wide', 'narrow'))
- reduce_bias_grad: float32 [768], P(('wide', 'narrow'))
- branch2_scale_grad: float32 [768], P(('wide', 'narrow'))
Inputs may be any that keep to these rules, and one draw needn't show every extreme that they name: `counts`: valid patches of each image, heavy-tailed; every draw holds full images and images with only 16 valid patches.
All inputs are finite; a program needn't handle non-finite values.
Results may differ from a plain program's by a relative error of at most 0.015.
Values may be sent and summed in bfloat16 or wider, within the bound.
No kernel may reach another device: no remote copies, remote signals or barrier semaphores. Data moves between devices by JAX's collectives and lax.ppermute only.
A program may use at most 192 MiB of HBM per device.

v0:
```python
from functools import partial
import jax
import jax.numpy as jnp
from jax import lax
from jax.sharding import PartitionSpec as P

HEADS = 12
HEAD = 64


def layer_norm(inputs, norm_gain, norm_shift):
    average = jnp.mean(inputs, axis=-1, keepdims=True)
    centered = inputs - average
    spread = jnp.mean(centered * centered, axis=-1, keepdims=True)
    return centered * lax.rsqrt(spread + 1e-06) * norm_gain + norm_shift


def contract_rows(left, right):
    return lax.dot_general(
        left, right, (((0,), (0,)), ((), ())), preferred_element_type=jnp.float32
    )


def contract_cols(left, right):
    return lax.dot_general(
        left, right, (((1,), (1,)), ((), ())), preferred_element_type=jnp.float32
    )


def column_sum(values):
    return jnp.sum(values.astype(jnp.float32), axis=0)


def regroup(gradient, wide_count, narrow_count):
    total_rows = gradient.shape[0]
    piece_rows = total_rows // (wide_count * narrow_count)
    split = gradient.reshape((wide_count, narrow_count, piece_rows) + gradient.shape[1:])
    return jnp.swapaxes(split, 0, 1).reshape(gradient.shape)


def per_device(
    patches,
    counts,
    cotangent,
    input_weight,
    output_weight,
    expand_weight,
    reduce_weight,
    norm1_gain,
    norm1_shift,
    query_bias,
    value_bias,
    output_bias,
    branch1_scale,
    norm2_gain,
    norm2_shift,
    expand_bias,
    reduce_bias,
    branch2_scale,
):
    whole = (
        lax.all_gather(input_weight, ("wide", "narrow"), axis=0, tiled=True),
        lax.all_gather(output_weight, ("wide", "narrow"), axis=0, tiled=True),
        lax.all_gather(expand_weight, ("wide", "narrow"), axis=0, tiled=True),
        lax.all_gather(reduce_weight, ("wide", "narrow"), axis=0, tiled=True),
        lax.all_gather(norm1_gain, ("wide", "narrow"), axis=0, tiled=True),
        lax.all_gather(norm1_shift, ("wide", "narrow"), axis=0, tiled=True),
        lax.all_gather(query_bias, ("wide", "narrow"), axis=0, tiled=True),
        lax.all_gather(value_bias, ("wide", "narrow"), axis=0, tiled=True),
        lax.all_gather(output_bias, ("wide", "narrow"), axis=0, tiled=True),
        lax.all_gather(branch1_scale, ("wide", "narrow"), axis=0, tiled=True),
        lax.all_gather(norm2_gain, ("wide", "narrow"), axis=0, tiled=True),
        lax.all_gather(norm2_shift, ("wide", "narrow"), axis=0, tiled=True),
        lax.all_gather(expand_bias, ("wide", "narrow"), axis=0, tiled=True),
        lax.all_gather(reduce_bias, ("wide", "narrow"), axis=0, tiled=True),
        lax.all_gather(branch2_scale, ("wide", "narrow"), axis=0, tiled=True),
    )
    w_input, w_output, w_expand, w_reduce = (whole[0], whole[1], whole[2], whole[3])
    (
        gain_one,
        shift_one,
        bias_query,
        bias_value,
        bias_output,
        scale_one,
        gain_two,
        shift_two,
        bias_expand,
        bias_reduce,
        scale_two,
    ) = tuple((item.astype(jnp.float32) for item in whole[4:]))
    n_images, n_patch, width = patches.shape
    n_rows = n_images * n_patch
    head_shape = (n_images, n_patch, HEADS, HEAD)
    score_scale = HEAD ** (-0.5)
    position = jnp.arange(n_patch, dtype=jnp.int32)
    valid_keys = position[None, :] < counts[:, None]
    row_mask = jnp.where(valid_keys, 1.0, 0.0).astype(jnp.float32).reshape(n_rows, 1)
    rows_in = patches.astype(jnp.float32).reshape(n_rows, width)
    normed_low = layer_norm(rows_in, gain_one, shift_one).astype(jnp.bfloat16)
    projections = jnp.dot(normed_low, w_input, preferred_element_type=jnp.float32)
    queries = (projections[:, :width] + bias_query).astype(jnp.bfloat16).reshape(head_shape)
    key_rows = projections[:, width : 2 * width].astype(jnp.bfloat16).reshape(head_shape)
    values = (projections[:, 2 * width :] + bias_value).astype(jnp.bfloat16).reshape(head_shape)

    def attention_scores():
        raw_scores = jnp.einsum(
            "iphd,iqhd->ihpq", queries, key_rows, preferred_element_type=jnp.float32
        )
        return jnp.where(valid_keys[:, None, None, :], raw_scores * score_scale, -1e30)

    scores = attention_scores()
    log_total = jax.nn.logsumexp(scores, axis=-1, keepdims=True)
    soft_low = jnp.exp(scores - log_total).astype(jnp.bfloat16)
    attended = jnp.einsum("ihpq,iqhd->iphd", soft_low, values, preferred_element_type=jnp.float32)
    attended_low = attended.astype(jnp.bfloat16).reshape(n_rows, width)
    projected = jnp.dot(attended_low, w_output, preferred_element_type=jnp.float32) + bias_output
    middle = rows_in + scale_one * projected
    second_low = layer_norm(middle, gain_two, shift_two).astype(jnp.bfloat16)
    hidden = jnp.dot(second_low, w_expand, preferred_element_type=jnp.float32) + bias_expand
    activated_low = jax.nn.gelu(hidden, approximate=False).astype(jnp.bfloat16)
    branch = jnp.dot(activated_low, w_reduce, preferred_element_type=jnp.float32) + bias_reduce
    outputs = middle + scale_two * branch
    again = (
        lax.all_gather(input_weight, ("wide", "narrow"), axis=0, tiled=True),
        lax.all_gather(output_weight, ("wide", "narrow"), axis=0, tiled=True),
        lax.all_gather(expand_weight, ("wide", "narrow"), axis=0, tiled=True),
        lax.all_gather(reduce_weight, ("wide", "narrow"), axis=0, tiled=True),
    )
    back_input, back_output, back_expand, back_reduce = (again[0], again[1], again[2], again[3])
    grad_out = cotangent.astype(jnp.float32).reshape(n_rows, width) * row_mask
    grad_branch = (grad_out * scale_two).astype(jnp.bfloat16)
    grad_scale_two = jnp.sum(grad_out * branch, axis=0)
    grad_bias_reduce = column_sum(grad_branch)
    grad_w_reduce = contract_rows(activated_low, grad_branch)
    grad_activated = contract_cols(grad_branch, back_reduce)
    gelu_exact = partial(jax.nn.gelu, approximate=False)
    _, gelu_back = jax.vjp(gelu_exact, hidden)
    grad_hidden = gelu_back(grad_activated)[0].astype(jnp.bfloat16)
    grad_bias_expand = column_sum(grad_hidden)
    grad_w_expand = contract_rows(second_low, grad_hidden)
    grad_second = contract_cols(grad_hidden, back_expand)
    _, norm_back_two = jax.vjp(layer_norm, middle, gain_two, shift_two)
    grad_middle, grad_gain_two, grad_shift_two = norm_back_two(grad_second)
    grad_middle = grad_middle + grad_out
    grad_projected = (grad_middle * scale_one).astype(jnp.bfloat16)
    grad_scale_one = jnp.sum(grad_middle * projected, axis=0)
    grad_bias_output = column_sum(grad_projected)
    grad_w_output = contract_rows(attended_low, grad_projected)
    grad_attended = (
        contract_cols(grad_projected, back_output).astype(jnp.bfloat16).reshape(head_shape)
    )
    scores = attention_scores()
    soft_full = jnp.exp(scores - log_total)
    soft_again = soft_full.astype(jnp.bfloat16)
    grad_soft = jnp.einsum(
        "iphd,iqhd->ihpq", grad_attended, values, preferred_element_type=jnp.float32
    )
    grad_values = jnp.einsum(
        "ihpq,iphd->iqhd", soft_again, grad_attended, preferred_element_type=jnp.float32
    ).astype(jnp.bfloat16)
    grad_scores = (
        soft_full * (grad_soft - jnp.sum(soft_full * grad_soft, axis=-1, keepdims=True))
    ).astype(jnp.bfloat16)
    grad_queries = (
        (
            jnp.einsum("ihpq,iqhd->iphd", grad_scores, key_rows, preferred_element_type=jnp.float32)
            * score_scale
        )
        .astype(jnp.bfloat16)
        .reshape(n_rows, width)
    )
    grad_keys = (
        (
            jnp.einsum("ihpq,iphd->iqhd", grad_scores, queries, preferred_element_type=jnp.float32)
            * score_scale
        )
        .astype(jnp.bfloat16)
        .reshape(n_rows, width)
    )
    grad_values = grad_values.reshape(n_rows, width)
    grad_bias_query = column_sum(grad_queries)
    grad_bias_value = column_sum(grad_values)
    grad_projections = jnp.concatenate([grad_queries, grad_keys, grad_values], axis=1)
    grad_w_input = contract_rows(normed_low, grad_projections)
    grad_normed = contract_cols(grad_projections, back_input)
    _, norm_back_one = jax.vjp(layer_norm, rows_in, gain_one, shift_one)
    grad_rows, grad_gain_one, grad_shift_one = norm_back_one(grad_normed)
    input_grad = grad_rows + grad_middle
    wide_count = lax.axis_size("wide")
    narrow_count = lax.axis_size("narrow")
    (
        part_w_input,
        part_w_output,
        part_w_expand,
        part_w_reduce,
        part_gain_one,
        part_shift_one,
        part_bias_query,
        part_bias_value,
        part_bias_output,
        part_scale_one,
        part_gain_two,
        part_shift_two,
        part_bias_expand,
        part_bias_reduce,
        part_scale_two,
    ) = tuple(
        (
            regroup(item, wide_count, narrow_count)
            for item in (
                grad_w_input,
                grad_w_output,
                grad_w_expand,
                grad_w_reduce,
                grad_gain_one,
                grad_shift_one,
                grad_bias_query,
                grad_bias_value,
                grad_bias_output,
                grad_scale_one,
                grad_gain_two,
                grad_shift_two,
                grad_bias_expand,
                grad_bias_reduce,
                grad_scale_two,
            )
        )
    )
    inner = (
        lax.psum_scatter(
            part_w_input.astype(jnp.bfloat16), "narrow", scatter_dimension=0, tiled=True
        ).astype(jnp.float32),
        lax.psum_scatter(
            part_w_output.astype(jnp.bfloat16), "narrow", scatter_dimension=0, tiled=True
        ).astype(jnp.float32),
        lax.psum_scatter(
            part_w_expand.astype(jnp.bfloat16), "narrow", scatter_dimension=0, tiled=True
        ).astype(jnp.float32),
        lax.psum_scatter(
            part_w_reduce.astype(jnp.bfloat16), "narrow", scatter_dimension=0, tiled=True
        ).astype(jnp.float32),
        lax.psum_scatter(
            part_gain_one.astype(jnp.bfloat16), "narrow", scatter_dimension=0, tiled=True
        ).astype(jnp.float32),
        lax.psum_scatter(
            part_shift_one.astype(jnp.bfloat16), "narrow", scatter_dimension=0, tiled=True
        ).astype(jnp.float32),
        lax.psum_scatter(
            part_bias_query.astype(jnp.bfloat16), "narrow", scatter_dimension=0, tiled=True
        ).astype(jnp.float32),
        lax.psum_scatter(
            part_bias_value.astype(jnp.bfloat16), "narrow", scatter_dimension=0, tiled=True
        ).astype(jnp.float32),
        lax.psum_scatter(
            part_bias_output.astype(jnp.bfloat16), "narrow", scatter_dimension=0, tiled=True
        ).astype(jnp.float32),
        lax.psum_scatter(
            part_scale_one.astype(jnp.bfloat16), "narrow", scatter_dimension=0, tiled=True
        ).astype(jnp.float32),
        lax.psum_scatter(
            part_gain_two.astype(jnp.bfloat16), "narrow", scatter_dimension=0, tiled=True
        ).astype(jnp.float32),
        lax.psum_scatter(
            part_shift_two.astype(jnp.bfloat16), "narrow", scatter_dimension=0, tiled=True
        ).astype(jnp.float32),
        lax.psum_scatter(
            part_bias_expand.astype(jnp.bfloat16), "narrow", scatter_dimension=0, tiled=True
        ).astype(jnp.float32),
        lax.psum_scatter(
            part_bias_reduce.astype(jnp.bfloat16), "narrow", scatter_dimension=0, tiled=True
        ).astype(jnp.float32),
        lax.psum_scatter(
            part_scale_two.astype(jnp.bfloat16), "narrow", scatter_dimension=0, tiled=True
        ).astype(jnp.float32),
    )
    summed = (
        lax.psum_scatter(inner[0], "wide", scatter_dimension=0, tiled=True),
        lax.psum_scatter(inner[1], "wide", scatter_dimension=0, tiled=True),
        lax.psum_scatter(inner[2], "wide", scatter_dimension=0, tiled=True),
        lax.psum_scatter(inner[3], "wide", scatter_dimension=0, tiled=True),
        lax.psum_scatter(inner[4], "wide", scatter_dimension=0, tiled=True),
        lax.psum_scatter(inner[5], "wide", scatter_dimension=0, tiled=True),
        lax.psum_scatter(inner[6], "wide", scatter_dimension=0, tiled=True),
        lax.psum_scatter(inner[7], "wide", scatter_dimension=0, tiled=True),
        lax.psum_scatter(inner[8], "wide", scatter_dimension=0, tiled=True),
        lax.psum_scatter(inner[9], "wide", scatter_dimension=0, tiled=True),
        lax.psum_scatter(inner[10], "wide", scatter_dimension=0, tiled=True),
        lax.psum_scatter(inner[11], "wide", scatter_dimension=0, tiled=True),
        lax.psum_scatter(inner[12], "wide", scatter_dimension=0, tiled=True),
        lax.psum_scatter(inner[13], "wide", scatter_dimension=0, tiled=True),
        lax.psum_scatter(inner[14], "wide", scatter_dimension=0, tiled=True),
    )
    return (
        outputs.reshape(n_images, n_patch, width).astype(jnp.bfloat16),
        input_grad.reshape(n_images, n_patch, width),
        summed[0],
        summed[1],
        summed[2],
        summed[3],
        summed[4],
        summed[5],
        summed[6],
        summed[7],
        summed[8],
        summed[9],
        summed[10],
        summed[11],
        summed[12],
        summed[13],
        summed[14],
    )


def solution(mesh):
    placed = (
        P(("wide", "narrow"), None, None),
        P(("wide", "narrow")),
        P(("wide", "narrow"), None, None),
        P(("wide", "narrow"), None),
        P(("wide", "narrow"), None),
        P(("wide", "narrow"), None),
        P(("wide", "narrow"), None),
        P(("wide", "narrow")),
        P(("wide", "narrow")),
        P(("wide", "narrow")),
        P(("wide", "narrow")),
        P(("wide", "narrow")),
        P(("wide", "narrow")),
        P(("wide", "narrow")),
        P(("wide", "narrow")),
        P(("wide", "narrow")),
        P(("wide", "narrow")),
        P(("wide", "narrow")),
    )
    return jax.shard_map(
        per_device,
        mesh=mesh,
        in_specs=placed,
        out_specs=(
            P(("wide", "narrow"), None, None),
            P(("wide", "narrow"), None, None),
            P(("wide", "narrow"), None),
            P(("wide", "narrow"), None),
            P(("wide", "narrow"), None),
            P(("wide", "narrow"), None),
            P(("wide", "narrow")),
            P(("wide", "narrow")),
            P(("wide", "narrow")),
            P(("wide", "narrow")),
            P(("wide", "narrow")),
            P(("wide", "narrow")),
            P(("wide", "narrow")),
            P(("wide", "narrow")),
            P(("wide", "narrow")),
            P(("wide", "narrow")),
            P(("wide", "narrow")),
        ),
        check_vma=False,
    )
```

profile of v0, /device:TPU:0, one launch (start us, length us, event | category | flops | bytes accessed | tf_op | source)
XLA Modules:
  0.0 793.1 jit_solution(13559499145613062602)
XLA Ops:
  12.1 1.8 convert_reduce_fusion
  13.9 2.0 fusion.44
  25.2 43.4 %all-reduce.34 = (bf16[768]{0:T(1024)(128)(2,1)S(1)}, bf16[768]{0:T(1024)(128)(2,1)S(1)}, bf16[768]{0:T(1024)(128)(2,1)S(1)}, bf16[768]{0:T(1024)(128)(2,1)S(1)}...) all-reduce(bf16[768]{0:T(1024)(128)(2,1)S(1)} %dynamic-update-slice, ...), channel_id=1, replica_groups=mesh['wide'=8,'narrow'=4] {'wide','narrow'}, use_global_device_ids=true, to_apply=%add.2 | all-reduce | flops 10752 | bytes 43008
  68.8 1.8 fusion.40
  70.6 2.6 copy.142
  73.2 1.6 multiply_convert_fusion.7
  74.8 6.3 fusion.90
  82.4 1.8 fusion.32
  84.2 1.6 copy.120
  85.8 2.9 reshape.301
  88.7 3.2 copy.121
  91.9 3.9 reshape.302
  95.8 2.6 copy.119
  98.4 3.9 reshape.300
  102.2 4.5 fusion.23
  106.8 3.9 exponential_reduce_fusion
  111.5 3.5 fusion.51
  116.7 12.8 %all-gather.7.cloned.1.call-done = bf16[768,768]{1,0:T(8,128)(2,1)} async-done(((bf16[24,768]{1,0:T(8,128)(2,1)}), bf16[768,768]{1,0:T(8,128)(2,1)}) %all-gather.7.cloned.1.call-update) | async-done | bytes 1179664 | tf_op jit(solution)/shard_map/all_gather | solution.py:63
  129.5 4.6 fusion.86
  134.2 1.7 copy-done.8
  136.4 58.6 %all-gather.9.cloned.1.call-done = bf16[768,3072]{1,0:T(8,128)(2,1)} async-done(((bf16[24,3072]{1,0:T(8,128)(2,1)}), bf16[768,3072]{1,0:T(8,128)(2,1)}) %all-gather.9.cloned.1.call-update) | async-done | bytes 4718608 | tf_op jit(solution)/shard_map/all_gather | solution.py:64
  194.9 36.6 %fusion = (f32[1024,3072]{1,0:T(8,128)}, f32[1024,3072]{1,0:T(8,128)}) fusion(f32[3072]{0:T(1024)S(1)} %convert_element_type.344, bf16[768,3072]{1,0:T(8,128)(2,1)} %all-gather.9.cloned.1.call-done, f32[1024,768]{1,0:T(8,128)} %copy-done.8, f32[768]{0:T(1024)S(1)} %convert_element_type.342, f32[768]{0:T(1024)S(1)} %convert_element_type.341, ...), kind=kOutput, calls=%fused_computation.2 | convolution fusion | flops 5033951232 | bytes 33056768 | tf_op jit(solution)/shard_map/dot_general | solution.py:120
  231.5 28.1 %all-gather.11.cloned.1.call-done = bf16[3072,768]{1,0:T(8,128)(2,1)} async-done(((bf16[96,768]{1,0:T(8,128)(2,1)}), bf16[3072,768]{1,0:T(8,128)(2,1)}) %all-gather.11.cloned.1.call-update) | async-done | bytes 4718608 | tf_op jit(solution)/shard_map/all_gather | solution.py:65
  259.7 16.9 %fusion.89 = (bf16[3072]{0:T(1024)(128)(2,1)S(1)}, bf16[1024,3072]{1,0:T(8,128)(2,1)}) fusion(f32[1024,3072]{1,0:T(8,128)} %get-tuple-element.78, bf16[1024,768]{1,0:T(8,128)(2,1)S(1)} %copy-done.15, bf16[3072,768]{1,0:T(8,128)(2,1)} %all-gather.11.cloned.1.call-done, f32[1024,3072]{1,0:T(8,128)} %get-tuple-element.79, f32[3072]{0:T(1024)S(1)} %convert_element_type.344), kind=kOutput, calls=%fused_computation.157 | convolution fusion | flops 4882166784 | bytes 37767168 | tf_op jit(solution)/shard_map/dot_general | solution.py:25
  276.5 9.4 %multiply_reduce_fusion.2 = (bf16[768]{0:T(1024)(128)(2,1)S(1)}, f32[1024]{0:T(1024)S(1)}, bf16[768]{0:T(1024)(128)(2,1)S(1)}, f32[1024,768]{1,0:T(8,128)S(1)}) fusion(f32[1024,768]{1,0:T(8,128)S(1)} %copy-done.9, f32[1024]{0:T(1024)S(1)} %fusion.70, f32[1024]{0:T(1024)S(1)} %broadcast_multiply_fusion, f32[768]{0:T(1024)S(1)} %convert_element_type.341, ...), kind=kOutput, calls=%fused_computation.80 | convolution fusion | flops 4838126592 | bytes 17319936 | tf_op jit(solution)/shard_map/dot_general | solution.py:25
  285.9 1.5 fusion.85
  288.2 1.8 copy-done.17
  290.0 1.4 fusion.55
  292.6 4.3 convolution_convert_fusion.4
  296.9 3.0 copy.127
  300.0 3.9 reshape.305
  303.8 11.0 %multiply_reduce_fusion = (f32[4,12,256]{2,1,0:T(8,128)S(1)}, f32[4,12,256,256]{2,3,1,0:T(8,128)}) fusion(f32[4,12,256,256]{2,3,1,0:T(8,128)} %copy-done, f32[4,12,256]{2,1,0:T(8,128)S(1)} %log_add_fusion, pred[4,256]{1,0:T(4,128)(4,1)S(1)} %iota_compare_fusion, bf16[4,256,12,64]{1,0,3,2:T(4,128)(2,1)S(1)} %copy-done.12, bf16[4,256,12,64]{1,0,3,2:T(4,128)(2,1)} %reshape.305), kind=kOutput, calls=%fused_computation.24 | convolution fusion | flops 418369536 | bytes 28410880 | tf_op jit(solution)/shard_map/iphd,iqhd->ihpq/dot_general | solution.py:156
  314.8 13.4 %multiply_convert_fusion = bf16[4,12,256,256]{2,3,1,0:T(8,128)(2,1)} fusion(f32[4,12,256,256]{2,3,1,0:T(8,128)} %get-tuple-element.82, f32[4,12,256,256]{2,3,1,0:T(8,128)} %copy-done, f32[4,12,256]{2,1,0:T(8,128)S(1)} %get-tuple-element.81, f32[4,12,256]{2,1,0:T(8,128)S(1)} %log_add_fusion, pred[4,256]{1,0:T(4,128)(4,1)S(1)} %iota_compare_fusion), kind=kLoop, calls=%fused_computation.23 | loop fusion | flops 18874368 | bytes 31556608 | tf_op jit(solution)/shard_map/convert_element_type | solution.py:164
  328.3 3.4 fusion.88
  332.9 1.5 copy.172
  334.4 2.6 copy.141
  337.0 4.8 fusion.54
  343.1 1.5 copy.171
  344.6 2.8 copy.140
  347.4 4.1 fusion.87
  352.7 1.5 copy.170
  354.2 1.7 copy.139
  355.9 6.7 fusion.29
  362.7 2.0 copy.143
  364.8 9.0 %convolution_convert_fusion = bf16[768,3072]{1,0:T(8,128)(2,1)S(1)} fusion(bf16[1024,3072]{1,0:T(8,128)(2,1)} %get-tuple-element.89, f32[1024,768]{1,0:T(8,128)} %copy-done.8, f32[768]{0:T(1024)S(1)} %convert_element_type.342, f32[768]{0:T(1024)S(1)} %convert_element_type.341, f32[1024]{0:T(1024)S(1)} %fusion.70, f32[1024]{0:T(1024)S(1)} %broadcast_multiply_fusion), kind=kOutput, calls=%fused_computation.50 | convolution fusion | flops 4838129664 | bytes 14170112 | tf_op jit(solution)/shard_map/dot_general | solution.py:19
  373.7 2.5 copy.145
  377.5 30.5 %fusion.3 = bf16[3072,1024]{0,1:T(8,128)(2,1)} fusion(f32[1024,3072]{1,0:T(8,128)} %get-tuple-element.79, f32[3072]{0:T(1024)S(1)} %convert_element_type.344), kind=kLoop, calls=%fused_computation.5 | loop fusion | flops 207618048 | bytes 18886656 | tf_op jit(solution)/shard_map/convert_element_type | solution.py:121
  408.0 8.9 %copy.146 = bf16[3072,1024]{1,0:T(8,128)(2,1)} copy(bf16[3072,1024]{0,1:T(8,128)(2,1)} %fusion.3) | data formatting | bytes 12582912 | tf_op jit(solution)/shard_map/convert_element_type | solution.py:121
  417.0 8.4 %convert_bitcast_fusion = bf16[4,8,96,768]{3,2,0,1:T(8,128)(2,1)S(1)} fusion(bf16[8,4,96,1024]{3,2,1,0:T(8,128)(2,1)} %bitcast.228, bf16[1024,768,1,1]{1,0,3,2:T(8,128)(2,1)S(1)} %bitcast.242), kind=kOutput, calls=%fused_computation.56 | convolution fusion | flops 4834197504 | bytes 12582912 | tf_op jit(solution)/shard_map/dot_general | solution.py:19
  425.4 2.5 copy.147
  428.0 1.8 convert_element_type.368
  430.0 2.6 convert_element_type.364
  432.6 21.4 %reduce-scatter.17.cloned.1.call-done = bf16[192,3072]{1,0:T(8,128)(2,1)} async-done(((bf16[768,3072]{1,0:T(8,128)(2,1)}), bf16[192,3072]{1,0:T(8,128)(2,1)}) %reduce-scatter.17.cloned.1.call-update) | async-done | bytes 1179664 | tf_op jit(solution)/shard_map/reduce_scatter | solution.py:237
  454.1 2.9 convert_element_type.373
  461.1 10.3 %fusion.82 = (bf16[768]{0:T(1024)(128)(2,1)S(1)}, f32[1024]{0:T(1024)S(1)}, f32[1024,768]{1,0:T(8,128)}) fusion(f32[768]{0:T(1024)S(1)} %copy-done.24, f32[1024]{0:T(1024)S(1)} %bitcast.244, bf16[4,256,768]{2,1,0:T(8,128)(2,1)S(1)} %copy-done.2, bf16[768,2304]{1,0:T(8,128)(2,1)} %all-gather.5.cloned.1.call-done, bf16[1024,768]{1,0:T(8,128)(2,1)} %copy.141, ...), kind=kOutput, calls=%fused_computation.150 | convolution fusion | flops 3642751232 | bytes 12988928 | tf_op jit(solution)/shard_map/dot_general | solution.py:25
  471.5 33.1 %reduce-scatter.21.cloned.1.call-done = bf16[768,768]{1,0:T(8,128)(2,1)} async-done(((bf16[3072,768]{1,0:T(8,128)(2,1)}), bf16[768,768]{1,0:T(8,128)(2,1)}) %reduce-scatter.21.cloned.1.call-update) | async-done | bytes 1179664 | tf_op jit(solution)/shard_map/reduce_scatter | solution.py:240
  504.6 2.9 convert_element_type.380
  507.5 3.2 fusion.41
  512.1 20.1 %multiply_reduce_fusion.1 = (bf16[768]{0:T(1024)(128)(2,1)S(1)}, bf16[768]{0:T(1024)(128)(2,1)S(1)}, f32[1024,768]{1,0:T(8,128)}, bf16[1024,768]{1,0:T(8,128)(2,1)}) fusion(bf16[4,256,768]{2,1,0:T(8,128)(2,1)S(1)} %copy-done.6, f32[1024]{0:T(1024)S(1)} %bitcast.249, f32[768]{0:T(1024)S(1)} %convert_element_type.346, f32[1024,768]{1,0:T(8,128)} %get-tuple-element.77, ...), kind=kOutput, calls=%fused_computation.79 | convolution fusion | flops 4861720576 | bytes 50383872 | tf_op jit(solution)/shard_map/dot_general | solution.py:122
  532.9 10.9 %all-reduce.35 = (bf16[768]{0:T(1024)(128)(2,1)S(1)}, bf16[768]{0:T(1024)(128)(2,1)S(1)}, bf16[768]{0:T(1024)(128)(2,1)S(1)}, bf16[768]{0:T(1024)(128)(2,1)S(1)}...) all-reduce(bf16[768]{0:T(1024)(128)(2,1)S(1)} %convert_element_type, ...), channel_id=10, replica_groups=mesh['wide'=8,'narrow'=4] {'narrow'}, use_global_device_ids=true, to_apply=%region_20.21.clone | all-reduce | flops 10752 | bytes 43008
  544.2 36.8 %all-reduce.33 = (f32[192]{0:T(256)S(1)}, f32[192]{0:T(256)S(1)}, f32[192]{0:T(256)S(1)}, f32[192]{0:T(256)S(1)}, f32[192]{0:T(256)S(1)}, /*index=5*/f32[192]{0:...) all-reduce(f32[192]{0:T(256)S(1)} %get-tuple-element.99, ...), channel_id=11, replica_groups=mesh['wide'=8,'narrow'=4] {'wide'}, use_global_device_ids=true, to_apply=%region_21.22.clone | all-reduce | flops 2688 | bytes 21504
  587.4 53.4 %reduce-scatter.11.cloned.1.call-done = f32[24,2304]{1,0:T(8,128)} async-done(((f32[192,2304]{1,0:T(8,128)}), f32[24,2304]{1,0:T(8,128)}) %reduce-scatter.11.cloned.1.call-update) | async-done | bytes 221200 | tf_op jit(solution)/shard_map/reduce_scatter | solution.py:278
  640.7 72.5 %reduce-scatter.19.cloned.1.call-done = f32[24,3072]{1,0:T(8,128)} async-done(((f32[192,3072]{1,0:T(8,128)}), f32[24,3072]{1,0:T(8,128)}) %reduce-scatter.19.cloned.1.call-update) | async-done | bytes 294928 | tf_op jit(solution)/shard_map/reduce_scatter | solution.py:280
  713.3 72.8 %reduce-scatter.23.cloned.1.call-done = f32[96,768]{1,0:T(8,128)} async-done(((f32[768,768]{1,0:T(8,128)}), f32[96,768]{1,0:T(8,128)}) %reduce-scatter.23.cloned.1.call-update) | async-done | bytes 294928 | tf_op jit(solution)/shard_map/reduce_scatter | solution.py:281
  (218 shorter events, 35.8 us)
Async XLA Ops:
  7.2 61.6 %copy-start.1 = (bf16[4,256,768]{2,1,0:T(8,128)(2,1)S(1)}, bf16[4,256,768]{2,1,0:T(8,128)(2,1)}, u32[]{:S(2)}) copy-start(bf16[4,256,768]{2,1,0:T(8,128)(2,1)} %param.18) | copy-start | bytes 4718596
  7.2 67.6 %all-gather.5.cloned.1.call-start = ((), (), s32[]{:S(2)}) async-start(), calls=%async_computation.8 | async-start | bytes 3649536 | tf_op jit(solution)/shard_map/all_gather | solution.py:62
  7.9 121.6 %all-gather.7.cloned.1.call-start = ((), (), s32[]{:S(2)}) async-start(), calls=%async_computation.9 | async-start | bytes 1216512 | tf_op jit(solution)/shard_map/all_gather | solution.py:63
  8.7 186.3 %all-gather.9.cloned.1.call-start = ((), (), s32[]{:S(2)}) async-start(), calls=%async_computation.10 | async-start | bytes 4866048 | tf_op jit(solution)/shard_map/all_gather | solution.py:64
  9.4 250.2 %all-gather.11.cloned.1.call-start = ((), (), s32[]{:S(2)}) async-start(), calls=%async_computation.11 | async-start | bytes 4866048 | tf_op jit(solution)/shard_map/all_gather | solution.py:65
  10.0 418.0 %reduce-scatter.13.cloned.1.call-start = ((), (), s32[]{:S(2)}) async-start(), calls=%async_computation.14 | async-start | bytes 1474560 | tf_op jit(solution)/shard_map/reduce_scatter | solution.py:234
  12.1 61.1 %copy-start.5 = (bf16[4,256,768]{2,1,0:T(8,128)(2,1)S(1)}, bf16[4,256,768]{2,1,0:T(8,128)(2,1)}, u32[]{:S(2)}) copy-start(bf16[4,256,768]{2,1,0:T(8,128)(2,1)} %param.20) | copy-start | bytes 4718596
  13.9 60.8 %copy-start.19 = (f32[1,2,4,128]{3,1,2,0:T(2,128)}, f32[1,2,4,128]{3,1,2,0:T(2,128)S(1)}, u32[]{:S(2)}) copy-start(f32[1,2,4,128]{3,1,2,0:T(2,128)S(1)} %copy.166) | copy-start | bytes 12292
  15.9 52.7 %copy-start.29 = (f32[1,2,4,128]{3,1,2,0:T(2,128)}, f32[1,2,4,128]{3,1,2,0:T(2,128)S(1)}, u32[]{:S(2)}) copy-start(f32[1,2,4,128]{3,1,2,0:T(2,128)S(1)} %copy.167) | copy-start | bytes 12292
  16.0 58.8 %copy-start.21 = (f32[1024]{0:T(1024)}, f32[1024]{0:T(1024)S(1)}, u32[]{:S(2)}) copy-start(f32[1024]{0:T(1024)S(1)} %rsqrt.22) | copy-start | bytes 12292
  68.6 6.1 copy-start.23
  68.7 6.1 copy-start.25
  68.7 60.8 %copy-start.32 = (f32[768]{0:T(1024)}, f32[768]{0:T(1024)S(1)}, u32[]{:S(2)}) copy-start(f32[768]{0:T(1024)S(1)} %convert_element_type.339) | copy-start | bytes 9220
  68.7 6.0 copy-start.27
  88.7 13.5 %copy-start.3 = (bf16[4,256,12,64]{1,0,3,2:T(4,128)(2,1)}, bf16[4,256,12,64]{1,0,3,2:T(4,128)(2,1)S(1)}, u32[]{:S(2)}) copy-start(bf16[4,256,12,64]{1,0,3,2:T(4,128)(2,1)S(1)} %reshape.301) | copy-start | bytes 4718596
  106.8 4.7 copy-start
  106.8 4.7 copy-start.11
  116.7 17.5 %copy-start.16 = (bf16[96,8,4,256]{3,1,2,0:T(8,128)(2,1)}, bf16[96,8,4,256]{3,1,2,0:T(8,128)(2,1)S(1)}, u32[]{:S(2)}) copy-start(bf16[96,8,4,256]{3,1,2,0:T(8,128)(2,1)S(1)} %copy.168) | copy-start | bytes 4718596
  134.1 1.7 copy-start.8
  136.4 123.3 %copy-start.15 = (bf16[1024,768]{1,0:T(8,128)(2,1)S(1)}, bf16[1024,768]{1,0:T(8,128)(2,1)}, u32[]{:S(2)}) copy-start(bf16[1024,768]{1,0:T(8,128)(2,1)} %multiply_convert_fusion.7) | copy-start | bytes 4718596
  259.7 16.9 %copy-start.9 = (f32[1024,768]{1,0:T(8,128)S(1)}, f32[1024,768]{1,0:T(8,128)}, u32[]{:S(2)}) copy-start(f32[1024,768]{1,0:T(8,128)} %copy-done.8) | copy-start | bytes 9437188
  285.9 1.6 copy-start.6
  285.9 1.6 copy-start.28
  287.4 4.0 copy-start.10
  287.4 2.6 copy-start.17
  288.2 4.3 copy-start.18
  292.6 137.4 %reduce-scatter.9.cloned.1.call-start = ((), (), s32[]{:S(2)}) async-start(), calls=%async_computation.12 | async-start | bytes 4423680 | tf_op jit(solution)/shard_map/reduce_scatter | solution.py:231
  296.9 6.9 copy-start.12
  303.8 24.4 %slice-start = ((s8[12582912]{0:T(1024)(128)(4,1)}), s8[4194304]{0:T(1024)(128)(4,1)S(1)}, s32[]{:S(2)}) async-start(s8[12582912]{0:T(1024)(128)(4,1)} %bitcast.223), calls=%async_computation.20 | async-start | bytes 8388608
  303.8 24.4 %slice-start.1 = ((s8[12582912]{0:T(1024)(128)(4,1)}), s8[4194304]{0:T(1024)(128)(4,1)S(1)}, s32[]{:S(2)}) async-start(s8[12582912]{0:T(1024)(128)(4,1)} %bitcast.223), calls=%async_computation.21 | async-start | bytes 8388608
  314.8 13.4 %slice-start.2 = ((s8[12582912]{0:T(1024)(128)(4,1)}), s8[4194304]{0:T(1024)(128)(4,1)S(1)}, s32[]{:S(2)}) async-start(s8[12582912]{0:T(1024)(128)(4,1)} %bitcast.223), calls=%async_computation.22 | async-start | bytes 8388608
  314.8 13.4 %copy-start.13 = (bf16[4,256,12,64]{1,0,3,2:T(4,128)(2,1)S(1)}, bf16[4,256,12,64]{1,0,3,2:T(4,128)(2,1)}, u32[]{:S(2)}) copy-start(bf16[4,256,12,64]{1,0,3,2:T(4,128)(2,1)} %reshape.305) | copy-start | bytes 4718596
  331.7 5.3 copy-start.4
  341.8 5.5 copy-start.7
  355.9 6.8 copy-start.14
  364.7 89.4 %reduce-scatter.17.cloned.1.call-start = ((), (), s32[]{:S(2)}) async-start(), calls=%async_computation.16 | async-start | bytes 5898240 | tf_op jit(solution)/shard_map/reduce_scatter | solution.py:237
  376.3 0.7 copy-start.26
  376.3 0.7 copy-start.31
  376.3 128.3 %reduce-scatter.21.cloned.1.call-start = ((), (), s32[]{:S(2)}) async-start(), calls=%async_computation.18 | async-start | bytes 5898240 | tf_op jit(solution)/shard_map/reduce_scatter | solution.py:240
  427.9 159.5 %reduce-scatter.15.cloned.1.call-start = ((), (), s32[]{:S(2)}) async-start(), calls=%async_computation.15 | async-start | bytes 663552 | tf_op jit(solution)/shard_map/reduce_scatter | solution.py:279
  429.8 27.2 %copy-start.36 = (u32[32]{0:T(128)S(1)}, u32[32]{0:T(128)}, u32[]{:S(2)}) copy-start(u32[32]{0:T(128)} %constant.159) | copy-start | bytes 388
  429.8 29.1 %copy-start.35 = (u32[32]{0:T(128)S(1)}, u32[32]{0:T(128)}, u32[]{:S(2)}) copy-start(u32[32]{0:T(128)} %constant.155) | copy-start | bytes 388
  429.9 31.0 %copy-start.34 = (bf16[768]{0:T(1024)(128)(2,1)S(1)}, bf16[768]{0:T(1024)(128)(2,1)}, u32[]{:S(2)}) copy-start(bf16[768]{0:T(1024)(128)(2,1)} %get-tuple-element.46) | copy-start | bytes 4612
  429.9 31.2 %copy-start.2 = (bf16[4,256,768]{2,1,0:T(8,128)(2,1)S(1)}, bf16[4,256,768]{2,1,0:T(8,128)(2,1)}, u32[]{:S(2)}) copy-start(bf16[4,256,768]{2,1,0:T(8,128)(2,1)} %param.18) | copy-start | bytes 4718596
  429.9 31.2 %copy-start.20 = (f32[1,2,4,128]{3,1,2,0:T(2,128)S(1)}, f32[1,2,4,128]{3,1,2,0:T(2,128)}, u32[]{:S(2)}) copy-start(f32[1,2,4,128]{3,1,2,0:T(2,128)} %copy-done.19) | copy-start | bytes 12292
  429.9 31.2 %copy-start.24 = (f32[768]{0:T(1024)S(1)}, f32[768]{0:T(1024)}, u32[]{:S(2)}) copy-start(f32[768]{0:T(1024)} %copy-done.23) | copy-start | bytes 9220
  429.9 210.8 %reduce-scatter.11.cloned.1.call-start = ((), (), s32[]{:S(2)}) async-start(), calls=%async_computation.13 | async-start | bytes 1990656 | tf_op jit(solution)/shard_map/reduce_scatter | solution.py:278
  432.6 280.7 %reduce-scatter.19.cloned.1.call-start = ((), (), s32[]{:S(2)}) async-start(), calls=%async_computation.17 | async-start | bytes 2654208 | tf_op jit(solution)/shard_map/reduce_scatter | solution.py:280
  457.0 329.1 %reduce-scatter.23.cloned.1.call-start = ((), (), s32[]{:S(2)}) async-start(), calls=%async_computation.19 | async-start | bytes 2654208 | tf_op jit(solution)/shard_map/reduce_scatter | solution.py:281
  461.1 10.3 %copy-start.30 = (f32[1,2,4,128]{3,1,2,0:T(2,128)S(1)}, f32[1,2,4,128]{3,1,2,0:T(2,128)}, u32[]{:S(2)}) copy-start(f32[1,2,4,128]{3,1,2,0:T(2,128)} %copy-done.29) | copy-start | bytes 12292
  471.4 36.0 %copy-start.22 = (f32[1024]{0:T(1024)S(1)}, f32[1024]{0:T(1024)}, u32[]{:S(2)}) copy-start(f32[1024]{0:T(1024)} %copy-done.21) | copy-start | bytes 12292
  471.4 40.6 %copy-start.33 = (f32[768]{0:T(1024)S(1)}, f32[768]{0:T(1024)}, u32[]{:S(2)}) copy-start(f32[768]{0:T(1024)} %copy-done.32) | copy-start | bytes 9220
Sparse Core Ops, SparseCore 0:
  10.9 62.9 all-gather.4
  76.8 52.6 all-gather.6
  132.4 62.4 all-gather.8
  197.7 61.9 all-gather.10
  292.7 23.8 reduce-scatter.12
  364.8 38.6 reduce-scatter.8
  406.1 47.9 reduce-scatter.16
  456.6 47.9 reduce-scatter.20
  508.4 62.6 reduce-scatter.14
  575.1 65.6 reduce-scatter.10
  644.8 68.4 reduce-scatter.18
  717.2 68.8 reduce-scatter.22
where the time goes:
time: 798 us; the launch traced here: 793 us
  waiting for transfers between devices  356 us (45%)
  matrix products  165 us (21%)
  blocking collectives  91.1 us (11%)
  local copies, waits for them, and re-layouts  86.7 us (11%)
  other arithmetic  76 us (10%)
  between operations  17.9 us (2%)
    unnamed x3, blocking collectives  91.1 us
    reduce_scatter x1, waiting for transfers between devices, per_device(): lax.psum_scatter(inner[3], 'wide', scatter_dimension=0, tiled=True)  72.8 us
    reduce_scatter x1, waiting for transfers between devices, per_device(): lax.psum_scatter(inner[2], 'wide', scatter_dimension=0, tiled=True)  72.5 us
    all_gather x1, waiting for transfers between devices, per_device(): lax.all_gather(expand_weight, ('wide', 'narrow'), axis=0, tiled=True)  58.6 us
    reduce_scatter x1, waiting for transfers between devices, per_device(): lax.psum_scatter(inner[0], 'wide', scatter_dimension=0, tiled=True)  53.4 us
    dot_general x4, matrix products, contract_cols(): lax.dot_general(left, right, (((1,), (1,)), ((), ())), preferred_element_...  40.9 us
    dot_general x1, matrix products, per_device(): jnp.dot(second_low, w_expand, preferred_element_type=jnp.float32)  36.6 us
    reduce_scatter x1, waiting for transfers between devices, per_device(): lax.psum_scatter(part_w_reduce.astype(jnp.bfloat16), 'narrow', scatter_di...  33.1 us
  transfers between devices with their start and end apart: 12, of which 8 were waited for; matrix products, arithmetic and copies ran while one was open for 37% of the time, Pallas kernels for 0%

commit v1 on v0

--- a/solution.py
+++ b/solution.py
@@ -58,11 +58,28 @@
     reduce_bias,
     branch2_scale,
 ):
+
+    def deliver_series_all(w_in):
+        along_axis = ("wide", "narrow")
+        found_now, spare = (lax.psum(1, axis_name=along_axis), lax.axis_index(along_axis))
+        raw_out, s_next = (w_in, 1)
+        while s_next < found_now:
+            big = lax.ppermute(
+                raw_out,
+                axis_name=along_axis,
+                perm=[(dev_j, dev_j ^ s_next) for dev_j in range(found_now)],
+            )
+            moved = jnp.concatenate([raw_out, big], axis=0)
+            kept_arr = jnp.concatenate([big, raw_out], axis=0)
+            raw_out = jnp.where(spare & s_next == 0, moved, kept_arr)
+            s_next = 2 * s_next
+        return raw_out
+
     whole = (
         lax.all_gather(input_weight, ("wide", "narrow"), axis=0, tiled=True),
         lax.all_gather(output_weight, ("wide", "narrow"), axis=0, tiled=True),
         lax.all_gather(expand_weight, ("wide", "narrow"), axis=0, tiled=True),
-        lax.all_gather(reduce_weight, ("wide", "narrow"), axis=0, tiled=True),
+        deliver_series_all(reduce_weight),
         lax.all_gather(norm1_gain, ("wide", "narrow"), axis=0, tiled=True),
         lax.all_gather(norm1_shift, ("wide", "narrow"), axis=0, tiled=True),
         lax.all_gather(query_bias, ("wide", "narrow"), axis=0, tiled=True),

time: 798 us -> 881 us (1.10)
  waiting for transfers between devices: 356 us -> 422 us
  matrix products: 165 us -> 178 us
    ppermute x0 -> x5, waiting for transfers between devices: none -> 133 us  [deliver_series_all(): lax.ppermute(raw_out, axis_name=along_axis, perm=[(dev_j, dev_j ^ s_next)...]
    reduce_scatter x1, waiting for transfers between devices: 33.1 us -> 0.02 us  [per_device(): lax.psum_scatter(part_w_reduce.astype(jnp.bfloat16), 'narrow', scatter_di...]
    reduce_scatter x1, waiting for transfers between devices: 53.4 us -> 23.7 us  [per_device(): lax.psum_scatter(inner[0], 'wide', scatter_dimension=0, tiled=True)]
    dot_general x1, matrix products: 3.53 us -> 13.8 us  [per_device(): jnp.einsum('ihpq,iqhd->iphd', soft_low, values, preferred_element_type=jn...]
    all_gather x1, waiting for transfers between devices: 12.8 us -> 3.54 us  [per_device(): lax.all_gather(output_weight, ('wide', 'narrow'), axis=0, tiled=True)]
    unnamed x122 -> x144, local copies, waits for them, and re-layouts: 26.7 us -> 19 us
  transfers between devices with their start and end apart: 12 -> 17, of which waited for: 8 -> 13; matrix products, arithmetic and copies ran while one was open for 37% -> 34% of each run, Pallas kernels for 0% -> 0%
where the time goes in v1:
time: 881 us; the launch traced here: 876 us
  waiting for transfers between devices  422 us (48%)
  matrix products  178 us (20%)
  blocking collectives  91.4 us (10%)
  other arithmetic  80.6 us (9%)
  local copies, waits for them, and re-layouts  79.2 us (9%)
  between operations  18 us (2%)
    ppermute x5, waiting for transfers between devices, deliver_series_all(): lax.ppermute(raw_out, axis_name=along_axis, perm=[(dev_j, dev_j ^ s_next)...  133 us
    unnamed x3, blocking collectives  91.4 us
    reduce_scatter x1, waiting for transfers between devices, per_device(): lax.psum_scatter(inner[3], 'wide', scatter_dimension=0, tiled=True)  72.9 us
    reduce_scatter x1, waiting for transfers between devices, per_device(): lax.psum_scatter(inner[2], 'wide', scatter_dimension=0, tiled=True)  72.6 us
    all_gather x1, waiting for transfers between devices, per_device(): lax.all_gather(expand_weight, ('wide', 'narrow'), axis=0, tiled=True)  58.5 us
    dot_general x4, matrix products, contract_cols(): lax.dot_general(left, right, (((1,), (1,)), ((), ())), preferred_element_...  39.2 us
    dot_general x1, matrix products, per_device(): jnp.dot(second_low, w_expand, preferred_element_type=jnp.float32)  36.6 us
    convert_element_type x1, other arithmetic, per_device(): activated_low = jax.nn.gelu(hidden, approximate=False).astype(jnp.bfloat16)  30 us
  transfers between devices with their start and end apart: 17, of which 13 were waited for; matrix products, arithmetic and copies ran while one was open for 34% of the time, Pallas kernels for 0%

profile of v1, /device:TPU:0, one launch (start us, length us, event | category | flops | bytes accessed | tf_op | source)
XLA Modules:
  0.0 875.7 jit_solution(4514804109947854899)
XLA Ops:
  12.2 1.7 convert_reduce_fusion
  13.9 2.0 fusion.50
  18.6 43.6 %all-reduce.34 = (bf16[768]{0:T(1024)(128)(2,1)S(1)}, bf16[768]{0:T(1024)(128)(2,1)S(1)}, bf16[768]{0:T(1024)(128)(2,1)S(1)}, bf16[768]{0:T(1024)(128)(2,1)S(1)}...) all-reduce(bf16[768]{0:T(1024)(128)(2,1)S(1)} %dynamic-update-slice, ...), channel_id=1, replica_groups=mesh['wide'=8,'narrow'=4] {'wide','narrow'}, use_global_device_ids=true, to_apply=%add.2 | all-reduce | flops 10752 | bytes 43008
  62.4 1.8 fusion.46
  64.2 2.6 copy.142
  68.3 5.6 all-gather.5.cloned.1.call-done
  74.0 6.3 fusion.97
  81.6 1.8 fusion.38
  83.3 1.7 copy.120
  85.0 2.9 reshape.301
  87.9 3.2 copy.121
  91.1 3.9 reshape.302
  95.0 2.6 copy.119
  97.6 3.9 reshape.300
  101.4 4.5 fusion.23
  106.0 3.8 exponential_reduce_fusion
  110.7 13.8 %fusion.57 = bf16[4,256,12,64]{1,3,2,0:T(8,128)(2,1)S(1)} fusion(bf16[4,256,12,64]{1,0,3,2:T(4,128)(2,1)S(1)} %copy-done.11, f32[4,12,256,256]{2,3,1,0:T(8,128)S(1)} %get-tuple-element.76, f32[4,12,256]{2,1,0:T(8,128)S(1)} %log_add_fusion, pred[4,256]{1,0:T(4,128)(4,1)S(1)} %iota_compare_fusion), kind=kOutput, calls=%fused_computation.108 | convolution fusion | flops 416022528 | bytes 15778816 | tf_op jit(solution)/shard_map/ihpq,iqhd->iphd/dot_general | solution.py:132
  126.2 3.5 all-gather.7.cloned.1.call-done
  129.7 4.6 fusion.93
  134.4 1.7 copy-done.8
  136.6 58.5 %all-gather.9.cloned.1.call-done = bf16[768,3072]{1,0:T(8,128)(2,1)} async-done(((bf16[24,3072]{1,0:T(8,128)(2,1)}), bf16[768,3072]{1,0:T(8,128)(2,1)}) %all-gather.9.cloned.1.call-update) | async-done | bytes 4718608 | tf_op jit(solution)/shard_map/all_gather | solution.py:81
  195.1 36.6 %fusion = (f32[1024,3072]{1,0:T(8,128)}, f32[1024,3072]{1,0:T(8,128)}) fusion(f32[3072]{0:T(1024)S(1)} %convert_element_type.344, bf16[768,3072]{1,0:T(8,128)(2,1)} %all-gather.9.cloned.1.call-done, f32[1024,768]{1,0:T(8,128)} %copy-done.8, f32[768]{0:T(1024)S(1)} %convert_element_type.342, f32[768]{0:T(1024)S(1)} %convert_element_type.341, ...), kind=kOutput, calls=%fused_computation.2 | convolution fusion | flops 5033951232 | bytes 33056768 | tf_op jit(solution)/shard_map/dot_general | solution.py:137
  231.7 28.1 %all-gather.11.cloned.1.call-done = bf16[3072,768]{1,0:T(8,128)(2,1)} async-done(((bf16[96,768]{1,0:T(8,128)(2,1)}), bf16[3072,768]{1,0:T(8,128)(2,1)}) %all-gather.11.cloned.1.call-update) | async-done | bytes 4718608 | tf_op jit(solution)/shard_map/all_gather | solution.py:145
  259.8 16.8 %fusion.96 = (bf16[3072]{0:T(1024)(128)(2,1)S(1)}, bf16[1024,3072]{1,0:T(8,128)(2,1)}) fusion(f32[1024,3072]{1,0:T(8,128)} %get-tuple-element.78, bf16[1024,768]{1,0:T(8,128)(2,1)S(1)} %copy-done.15, bf16[3072,768]{1,0:T(8,128)(2,1)} %all-gather.11.cloned.1.call-done, f32[1024,3072]{1,0:T(8,128)} %get-tuple-element.79, f32[3072]{0:T(1024)S(1)} %convert_element_type.344), kind=kOutput, calls=%fused_computation.169 | convolution fusion | flops 4882166784 | bytes 37767168 | tf_op jit(solution)/shard_map/dot_general | solution.py:25
  276.6 9.4 %multiply_reduce_fusion.2 = (bf16[768]{0:T(1024)(128)(2,1)S(1)}, f32[1024]{0:T(1024)S(1)}, bf16[768]{0:T(1024)(128)(2,1)S(1)}, f32[1024,768]{1,0:T(8,128)S(1)}) fusion(f32[1024,768]{1,0:T(8,128)S(1)} %copy-done.9, f32[1024]{0:T(1024)S(1)} %fusion.76, f32[1024]{0:T(1024)S(1)} %broadcast_multiply_fusion, f32[768]{0:T(1024)S(1)} %convert_element_type.341, ...), kind=kOutput, calls=%fused_computation.87 | convolution fusion | flops 4838126592 | bytes 17319936 | tf_op jit(solution)/shard_map/dot_general | solution.py:25
  288.4 1.8 copy-done.17
  292.8 3.8 convolution_convert_fusion.4
  296.6 3.1 copy.127
  299.7 3.9 reshape.305
  303.7 11.0 %multiply_reduce_fusion = (f32[4,12,256]{2,1,0:T(8,128)S(1)}, f32[4,12,256,256]{2,3,1,0:T(8,128)}) fusion(f32[4,12,256,256]{2,3,1,0:T(8,128)} %copy-done, f32[4,12,256]{2,1,0:T(8,128)S(1)} %log_add_fusion, pred[4,256]{1,0:T(4,128)(4,1)S(1)} %iota_compare_fusion, bf16[4,256,12,64]{1,0,3,2:T(4,128)(2,1)S(1)} %copy-done.12, bf16[4,256,12,64]{1,0,3,2:T(4,128)(2,1)} %reshape.305), kind=kOutput, calls=%fused_computation.24 | convolution fusion | flops 418369536 | bytes 28410880 | tf_op jit(solution)/shard_map/iphd,iqhd->ihpq/dot_general | solution.py:173
  314.6 13.4 %multiply_convert_fusion = bf16[4,12,256,256]{2,3,1,0:T(8,128)(2,1)} fusion(f32[4,12,256,256]{2,3,1,0:T(8,128)} %get-tuple-element.82, f32[4,12,256,256]{2,3,1,0:T(8,128)} %copy-done, f32[4,12,256]{2,1,0:T(8,128)S(1)} %get-tuple-element.81, f32[4,12,256]{2,1,0:T(8,128)S(1)} %log_add_fusion, pred[4,256]{1,0:T(4,128)(4,1)S(1)} %iota_compare_fusion), kind=kLoop, calls=%fused_computation.23 | loop fusion | flops 18874368 | bytes 31556608 | tf_op jit(solution)/shard_map/convert_element_type | solution.py:181
  328.1 3.4 fusion.95
  334.3 2.6 copy.141
  336.9 4.8 fusion.60
  344.4 2.8 copy.140
  347.2 4.1 fusion.94
  354.4 6.7 fusion.35
  361.1 2.0 copy.143
  363.1 9.0 %convolution_convert_fusion = bf16[768,3072]{1,0:T(8,128)(2,1)S(1)} fusion(bf16[1024,3072]{1,0:T(8,128)(2,1)} %get-tuple-element.89, f32[1024,768]{1,0:T(8,128)} %copy-done.8, f32[768]{0:T(1024)S(1)} %convert_element_type.342, f32[768]{0:T(1024)S(1)} %convert_element_type.341, f32[1024]{0:T(1024)S(1)} %fusion.76, f32[1024]{0:T(1024)S(1)} %broadcast_multiply_fusion), kind=kOutput, calls=%fused_computation.50 | convolution fusion | flops 4838129664 | bytes 14170112 | tf_op jit(solution)/shard_map/dot_general | solution.py:19
  372.1 2.5 copy.145
  375.9 30.0 %fusion.3 = bf16[3072,1024]{0,1:T(8,128)(2,1)} fusion(f32[1024,3072]{1,0:T(8,128)} %get-tuple-element.79, f32[3072]{0:T(1024)S(1)} %convert_element_type.344), kind=kLoop, calls=%fused_computation.5 | loop fusion | flops 207618048 | bytes 18886656 | tf_op jit(solution)/shard_map/convert_element_type | solution.py:138
  406.0 9.0 %copy.146 = bf16[3072,1024]{1,0:T(8,128)(2,1)} copy(bf16[3072,1024]{0,1:T(8,128)(2,1)} %fusion.3) | data formatting | bytes 12582912 | tf_op jit(solution)/shard_map/convert_element_type | solution.py:138
  415.0 8.5 convert_bitcast_fusion
  423.4 2.6 copy.147
  426.1 1.8 convert_element_type.368
  428.1 2.5 convert_element_type.364
  430.7 21.9 %reduce-scatter.17.cloned.1.call-done = bf16[192,3072]{1,0:T(8,128)(2,1)} async-done(((bf16[768,3072]{1,0:T(8,128)(2,1)}), bf16[192,3072]{1,0:T(8,128)(2,1)}) %reduce-scatter.17.cloned.1.call-update) | async-done | bytes 1179664 | tf_op jit(solution)/shard_map/reduce_scatter | solution.py:254
  452.6 2.9 convert_element_type.373
  457.5 8.7 collective-permute-done.1
  467.9 13.1 %collective-permute-done.2 = bf16[384,768]{1,0:T(8,128)(2,1)} collective-permute-done((bf16[384,768]{1,0:T(8,128)(2,1)S(1)}, bf16[384,768]{1,0:T(8,128)(2,1)}, u32[]{:S(2)}, u32[]{:S(2)}) %collective-permute-start.2) | collective-permute-done | bytes 589856 | tf_op jit(solution)/shard_map/ppermute | solution.py:67
  481.1 1.9 maximum_select_fusion.3
  484.5 24.9 %collective-permute-done.3 = bf16[768,768]{1,0:T(8,128)(2,1)} collective-permute-done((bf16[768,768]{1,0:T(8,128)(2,1)S(1)}, bf16[768,768]{1,0:T(8,128)(2,1)}, u32[]{:S(2)}, u32[]{:S(2)}) %collective-permute-start.3) | collective-permute-done | bytes 1179680 | tf_op jit(solution)/shard_map/ppermute | solution.py:67
  509.4 3.2 maximum_select_fusion.2
  512.7 2.5 collective-permute-start.4
  519.2 2.8 convert_element_type.380
  522.1 9.1 %fusion.89 = (bf16[768]{0:T(1024)(128)(2,1)S(1)}, f32[1024]{0:T(1024)S(1)}, f32[1024,768]{1,0:T(8,128)}) fusion(f32[768]{0:T(1024)S(1)} %copy-done.24, f32[1024]{0:T(1024)S(1)} %bitcast.243, bf16[4,256,768]{2,1,0:T(8,128)(2,1)S(1)} %copy-done.2, bf16[768,2304]{1,0:T(8,128)(2,1)} %all-gather.5.cloned.1.call-done, bf16[1024,768]{1,0:T(8,128)(2,1)} %copy.141, ...), kind=kOutput, calls=%fused_computation.162 | convolution fusion | flops 3642751232 | bytes 12988928 | tf_op jit(solution)/shard_map/dot_general | solution.py:25
  532.7 3.0 fusion.47
  535.7 84.6 %collective-permute-done.4 = bf16[1536,768]{1,0:T(8,128)(2,1)} collective-permute-done((bf16[1536,768]{1,0:T(8,128)(2,1)}, bf16[1536,768]{1,0:T(8,128)(2,1)}, u32[]{:S(2)}, u32[]{:S(2)}) %collective-permute-start.4) | collective-permute-done | bytes 2359328 | tf_op jit(solution)/shard_map/ppermute | solution.py:67
  620.3 23.8 %multiply_reduce_fusion.1 = (bf16[768]{0:T(1024)(128)(2,1)S(1)}, bf16[768]{0:T(1024)(128)(2,1)S(1)}, f32[1024,768]{1,0:T(8,128)}, bf16[1024,768]{1,0:T(8,128)(2,1)}) fusion(bf16[4,256,768]{2,1,0:T(8,128)(2,1)S(1)} %copy-done.6, f32[1024]{0:T(1024)S(1)} %bitcast.248, f32[768]{0:T(1024)S(1)} %convert_element_type.346, f32[1024,768]{1,0:T(8,128)} %get-tuple-element.77, ...), kind=kOutput, calls=%fused_computation.86 | convolution fusion | flops 4882954240 | bytes 50383872 | tf_op jit(solution)/shard_map/dot_general | solution.py:139
  644.8 10.7 %all-reduce.35 = (bf16[768]{0:T(1024)(128)(2,1)S(1)}, bf16[768]{0:T(1024)(128)(2,1)S(1)}, bf16[768]{0:T(1024)(128)(2,1)S(1)}, bf16[768]{0:T(1024)(128)(2,1)S(1)}...) all-reduce(bf16[768]{0:T(1024)(128)(2,1)S(1)} %convert_element_type, ...), channel_id=10, replica_groups=mesh['wide'=8,'narrow'=4] {'narrow'}, use_global_device_ids=true, to_apply=%region_20.21.clone | all-reduce | flops 10752 | bytes 43008
  655.9 37.1 %all-reduce.33 = (f32[192]{0:T(256)S(1)}, f32[192]{0:T(256)S(1)}, f32[192]{0:T(256)S(1)}, f32[192]{0:T(256)S(1)}, f32[192]{0:T(256)S(1)}, /*index=5*/f32[192]{0:...) all-reduce(f32[192]{0:T(256)S(1)} %get-tuple-element.99, ...), channel_id=11, replica_groups=mesh['wide'=8,'narrow'=4] {'wide'}, use_global_device_ids=true, to_apply=%region_21.22.clone | all-reduce | flops 2688 | bytes 21504
  699.4 23.7 %reduce-scatter.11.cloned.1.call-done = f32[24,2304]{1,0:T(8,128)} async-done(((f32[192,2304]{1,0:T(8,128)}), f32[24,2304]{1,0:T(8,128)}) %reduce-scatter.11.cloned.1.call-update) | async-done | bytes 221200 | tf_op jit(solution)/shard_map/reduce_scatter | solution.py:295
  723.1 72.6 %reduce-scatter.19.cloned.1.call-done = f32[24,3072]{1,0:T(8,128)} async-done(((f32[192,3072]{1,0:T(8,128)}), f32[24,3072]{1,0:T(8,128)}) %reduce-scatter.19.cloned.1.call-update) | async-done | bytes 294928 | tf_op jit(solution)/shard_map/reduce_scatter | solution.py:297
  795.7 72.9 %reduce-scatter.23.cloned.1.call-done = f32[96,768]{1,0:T(8,128)} async-done(((f32[768,768]{1,0:T(8,128)}), f32[96,768]{1,0:T(8,128)}) %reduce-scatter.23.cloned.1.call-update) | async-done | bytes 294928 | tf_op jit(solution)/shard_map/reduce_scatter | solution.py:298
  (254 shorter events, 43.9 us)
Async XLA Ops:
  7.2 55.2 %copy-start.1 = (bf16[4,256,768]{2,1,0:T(8,128)(2,1)S(1)}, bf16[4,256,768]{2,1,0:T(8,128)(2,1)}, u32[]{:S(2)}) copy-start(bf16[4,256,768]{2,1,0:T(8,128)(2,1)} %param.18) | copy-start | bytes 4718596
  7.2 8.8 %copy-start.35 = (bf16[24]{0:T(256)(128)(2,1)S(1)}, bf16[24]{0:T(256)(128)(2,1)}, u32[]{:S(2)}) copy-start(bf16[24]{0:T(256)(128)(2,1)} %param.34) | copy-start | bytes 148
  7.2 9.0 %copy-start.36 = (bf16[24]{0:T(256)(128)(2,1)S(1)}, bf16[24]{0:T(256)(128)(2,1)}, u32[]{:S(2)}) copy-start(bf16[24]{0:T(256)(128)(2,1)} %param.31) | copy-start | bytes 148
  7.2 9.3 %copy-start.37 = (bf16[24]{0:T(256)(128)(2,1)S(1)}, bf16[24]{0:T(256)(128)(2,1)}, u32[]{:S(2)}) copy-start(bf16[24]{0:T(256)(128)(2,1)} %param.32) | copy-start | bytes 148
  7.2 9.5 %copy-start.38 = (bf16[24]{0:T(256)(128)(2,1)S(1)}, bf16[24]{0:T(256)(128)(2,1)}, u32[]{:S(2)}) copy-start(bf16[24]{0:T(256)(128)(2,1)} %param.30) | copy-start | bytes 148
  7.2 9.7 %copy-start.39 = (bf16[24]{0:T(256)(128)(2,1)S(1)}, bf16[24]{0:T(256)(128)(2,1)}, u32[]{:S(2)}) copy-start(bf16[24]{0:T(256)(128)(2,1)} %param.29) | copy-start | bytes 148
  7.3 9.9 %copy-start.40 = (bf16[24]{0:T(256)(128)(2,1)S(1)}, bf16[24]{0:T(256)(128)(2,1)}, u32[]{:S(2)}) copy-start(bf16[24]{0:T(256)(128)(2,1)} %param.27) | copy-start | bytes 148
  7.3 10.2 %copy-start.41 = (bf16[24]{0:T(256)(128)(2,1)S(1)}, bf16[24]{0:T(256)(128)(2,1)}, u32[]{:S(2)}) copy-start(bf16[24]{0:T(256)(128)(2,1)} %param.28) | copy-start | bytes 148
  7.3 10.4 %copy-start.42 = (bf16[24]{0:T(256)(128)(2,1)S(1)}, bf16[24]{0:T(256)(128)(2,1)}, u32[]{:S(2)}) copy-start(bf16[24]{0:T(256)(128)(2,1)} %param.25) | copy-start | bytes 148
  7.3 10.6 %copy-start.43 = (bf16[24]{0:T(256)(128)(2,1)S(1)}, bf16[24]{0:T(256)(128)(2,1)}, u32[]{:S(2)}) copy-start(bf16[24]{0:T(256)(128)(2,1)} %param.26) | copy-start | bytes 148
  7.3 10.8 %copy-start.44 = (bf16[24]{0:T(256)(128)(2,1)S(1)}, bf16[24]{0:T(256)(128)(2,1)}, u32[]{:S(2)}) copy-start(bf16[24]{0:T(256)(128)(2,1)} %param.35) | copy-start | bytes 148
  7.3 11.1 %copy-start.45 = (bf16[96]{0:T(256)(128)(2,1)S(1)}, bf16[96]{0:T(256)(128)(2,1)}, u32[]{:S(2)}) copy-start(bf16[96]{0:T(256)(128)(2,1)} %param.33) | copy-start | bytes 580
  7.3 66.6 %all-gather.5.cloned.1.call-start = ((), (), s32[]{:S(2)}) async-start(), calls=%async_computation.8 | async-start | bytes 3649536 | tf_op jit(solution)/shard_map/all_gather | solution.py:79
  8.1 121.6 %all-gather.7.cloned.1.call-start = ((), (), s32[]{:S(2)}) async-start(), calls=%async_computation.9 | async-start | bytes 1216512 | tf_op jit(solution)/shard_map/all_gather | solution.py:80
  8.8 186.3 %all-gather.9.cloned.1.call-start = ((), (), s32[]{:S(2)}) async-start(), calls=%async_computation.10 | async-start | bytes 4866048 | tf_op jit(solution)/shard_map/all_gather | solution.py:81
  9.5 250.2 %all-gather.11.cloned.1.call-start = ((), (), s32[]{:S(2)}) async-start(), calls=%async_computation.11 | async-start | bytes 4866048 | tf_op jit(solution)/shard_map/all_gather | solution.py:145
  10.1 416.0 %reduce-scatter.13.cloned.1.call-start = ((), (), s32[]{:S(2)}) async-start(), calls=%async_computation.14 | async-start | bytes 1474560 | tf_op jit(solution)/shard_map/reduce_scatter | solution.py:251
  13.9 52.8 %copy-start.19 = (f32[1,2,4,128]{3,1,2,0:T(2,128)}, f32[1,2,4,128]{3,1,2,0:T(2,128)S(1)}, u32[]{:S(2)}) copy-start(f32[1,2,4,128]{3,1,2,0:T(2,128)S(1)} %copy.166) | copy-start | bytes 12292
  15.9 50.8 %copy-start.5 = (bf16[4,256,768]{2,1,0:T(8,128)(2,1)S(1)}, bf16[4,256,768]{2,1,0:T(8,128)(2,1)}, u32[]{:S(2)}) copy-start(bf16[4,256,768]{2,1,0:T(8,128)(2,1)} %param.20) | copy-start | bytes 4718596
  16.0 46.3 %copy-start.29 = (f32[1,2,4,128]{3,1,2,0:T(2,128)}, f32[1,2,4,128]{3,1,2,0:T(2,128)S(1)}, u32[]{:S(2)}) copy-start(f32[1,2,4,128]{3,1,2,0:T(2,128)S(1)} %copy.167) | copy-start | bytes 12292
  16.0 52.4 %copy-start.21 = (f32[1024]{0:T(1024)}, f32[1024]{0:T(1024)S(1)}, u32[]{:S(2)}) copy-start(f32[1024]{0:T(1024)S(1)} %rsqrt.22) | copy-start | bytes 12292
  62.2 6.1 copy-start.23
  62.2 6.1 copy-start.25
  62.3 67.4 %copy-start.32 = (f32[768]{0:T(1024)}, f32[768]{0:T(1024)S(1)}, u32[]{:S(2)}) copy-start(f32[768]{0:T(1024)S(1)} %convert_element_type.339) | copy-start | bytes 9220
  62.3 6.0 copy-start.27
  87.9 13.5 %copy-start.3 = (bf16[4,256,12,64]{1,0,3,2:T(4,128)(2,1)}, bf16[4,256,12,64]{1,0,3,2:T(4,128)(2,1)S(1)}, u32[]{:S(2)}) copy-start(bf16[4,256,12,64]{1,0,3,2:T(4,128)(2,1)S(1)} %reshape.301) | copy-start | bytes 4718596
  106.0 4.8 copy-start
  106.0 4.7 copy-start.11
  126.1 8.2 copy-start.16
  134.3 1.7 copy-start.8
  136.6 123.2 %copy-start.15 = (bf16[1024,768]{1,0:T(8,128)(2,1)S(1)}, bf16[1024,768]{1,0:T(8,128)(2,1)}, u32[]{:S(2)}) copy-start(bf16[1024,768]{1,0:T(8,128)(2,1)} %multiply_convert_fusion.7) | copy-start | bytes 4718596
  259.8 16.9 %copy-start.9 = (f32[1024,768]{1,0:T(8,128)S(1)}, f32[1024,768]{1,0:T(8,128)}, u32[]{:S(2)}) copy-start(f32[1024,768]{1,0:T(8,128)} %copy-done.8) | copy-start | bytes 9437188
  286.0 1.6 copy-start.6
  287.6 4.0 copy-start.10
  287.6 2.5 copy-start.17
  292.8 135.3 %reduce-scatter.9.cloned.1.call-start = ((), (), s32[]{:S(2)}) async-start(), calls=%async_computation.12 | async-start | bytes 4423680 | tf_op jit(solution)/shard_map/reduce_scatter | solution.py:248
  296.6 7.0 copy-start.12
  303.7 24.4 %slice-start = ((s8[12582912]{0:T(1024)(128)(4,1)}), s8[4194304]{0:T(1024)(128)(4,1)S(1)}, s32[]{:S(2)}) async-start(s8[12582912]{0:T(1024)(128)(4,1)} %bitcast.222), calls=%async_computation.20 | async-start | bytes 8388608
  303.7 24.4 %slice-start.1 = ((s8[12582912]{0:T(1024)(128)(4,1)}), s8[4194304]{0:T(1024)(128)(4,1)S(1)}, s32[]{:S(2)}) async-start(s8[12582912]{0:T(1024)(128)(4,1)} %bitcast.222), calls=%async_computation.21 | async-start | bytes 8388608
  314.6 13.4 %slice-start.2 = ((s8[12582912]{0:T(1024)(128)(4,1)}), s8[4194304]{0:T(1024)(128)(4,1)S(1)}, s32[]{:S(2)}) async-start(s8[12582912]{0:T(1024)(128)(4,1)} %bitcast.222), calls=%async_computation.22 | async-start | bytes 8388608
  314.6 13.4 %copy-start.13 = (bf16[4,256,12,64]{1,0,3,2:T(4,128)(2,1)S(1)}, bf16[4,256,12,64]{1,0,3,2:T(4,128)(2,1)}, u32[]{:S(2)}) copy-start(bf16[4,256,12,64]{1,0,3,2:T(4,128)(2,1)} %reshape.305) | copy-start | bytes 4718596
  332.8 4.1 copy-start.4
  342.9 4.3 copy-start.7
  363.1 89.5 %reduce-scatter.17.cloned.1.call-start = ((), (), s32[]{:S(2)}) async-start(), calls=%async_computation.16 | async-start | bytes 5898240 | tf_op jit(solution)/shard_map/reduce_scatter | solution.py:254
  374.7 144.5 %reduce-scatter.21.cloned.1.call-start = ((), (), s32[]{:S(2)}) async-start(), calls=%async_computation.18 | async-start | bytes 5898240 | tf_op jit(solution)/shard_map/reduce_scatter | solution.py:257
  426.1 273.4 %reduce-scatter.15.cloned.1.call-start = ((), (), s32[]{:S(2)}) async-start(), calls=%async_computation.15 | async-start | bytes 663552 | tf_op jit(solution)/shard_map/reduce_scatter | solution.py:296
  428.0 295.1 %reduce-scatter.11.cloned.1.call-start = ((), (), s32[]{:S(2)}) async-start(), calls=%async_computation.13 | async-start | bytes 1990656 | tf_op jit(solution)/shard_map/reduce_scatter | solution.py:295
  430.6 25.0 %copy-start.18 = (bf16[96,768]{1,0:T(8,128)(2,1)S(1)}, bf16[96,768]{1,0:T(8,128)(2,1)}, u32[]{:S(2)}) copy-start(bf16[96,768]{1,0:T(8,128)(2,1)} %param.24) | copy-start | bytes 442372
  430.6 365.1 %reduce-scatter.19.cloned.1.call-start = ((), (), s32[]{:S(2)}) async-start(), calls=%async_computation.17 | async-start | bytes 2654208 | tf_op jit(solution)/shard_map/reduce_scatter | solution.py:297
  455.5 413.1 %reduce-scatter.23.cloned.1.call-start = ((), (), s32[]{:S(2)}) async-start(), calls=%async_computation.19 | async-start | bytes 2654208 | tf_op jit(solution)/shard_map/reduce_scatter | solution.py:298
  455.6 1.4 collective-permute-start
  457.1 9.1 %collective-permute-start.1 = (bf16[192,768]{1,0:T(8,128)(2,1)S(1)}, bf16[192,768]{1,0:T(8,128)(2,1)S(1)}, u32[]{:S(2)}, u32[]{:S(2)}) collective-permute-start(bf16[192,768]{1,0:T(8,128)(2,1)S(1)} %maximum_select_fusion.5), channel_id=1, source_target_pairs={{0,2},{1,3},{2,0},{3,1},{4,6},{5,7},{6,4},{7,5},{8,10},{9,11},{10,... | collective-permute-start | bytes 884744 | tf_op jit(solution)/shard_map/ppermute | solution.py:67
  466.4 14.7 %collective-permute-start.2 = (bf16[384,768]{1,0:T(8,128)(2,1)S(1)}, bf16[384,768]{1,0:T(8,128)(2,1)}, u32[]{:S(2)}, u32[]{:S(2)}) collective-permute-start(bf16[384,768]{1,0:T(8,128)(2,1)S(1)} %maximum_select_fusion.4), channel_id=1, source_target_pairs={{0,4},{1,5},{2,6},{3,7},{4,0},{5,1},{6,2},{7,3},{8,12},{9,13},{10,... | collective-permute-start | bytes 1769480 | tf_op jit(solution)/shard_map/ppermute | solution.py:67
  467.9 47.2 %copy-start.47 = (u32[32]{0:T(128)S(1)}, u32[32]{0:T(128)}, u32[]{:S(2)}) copy-start(u32[32]{0:T(128)} %constant.180) | copy-start | bytes 388
  467.9 49.1 %copy-start.46 = (u32[32]{0:T(128)S(1)}, u32[32]{0:T(128)}, u32[]{:S(2)}) copy-start(u32[32]{0:T(128)} %constant.176) | copy-start | bytes 388
  467.9 51.0 %copy-start.34 = (bf16[768]{0:T(1024)(128)(2,1)S(1)}, bf16[768]{0:T(1024)(128)(2,1)}, u32[]{:S(2)}) copy-start(bf16[768]{0:T(1024)(128)(2,1)} %get-tuple-element.46) | copy-start | bytes 4612
  483.0 26.5 %collective-permute-start.3 = (bf16[768,768]{1,0:T(8,128)(2,1)S(1)}, bf16[768,768]{1,0:T(8,128)(2,1)}, u32[]{:S(2)}, u32[]{:S(2)}) collective-permute-start(bf16[768,768]{1,0:T(8,128)(2,1)S(1)} %maximum_select_fusion.3), channel_id=1, source_target_pairs={{0,8},{1,9},{2,10},{3,11},{4,12},{5,13},{6,14},{7,15},{8,0},{9,1},... | collective-permute-start | bytes 3538952 | tf_op jit(solution)/shard_map/ppermute | solution.py:67
  512.7 9.4 %copy-start.2 = (bf16[4,256,768]{2,1,0:T(8,128)(2,1)S(1)}, bf16[4,256,768]{2,1,0:T(8,128)(2,1)}, u32[]{:S(2)}) copy-start(bf16[4,256,768]{2,1,0:T(8,128)(2,1)} %param.18) | copy-start | bytes 4718596
  512.7 9.4 %copy-start.20 = (f32[1,2,4,128]{3,1,2,0:T(2,128)S(1)}, f32[1,2,4,128]{3,1,2,0:T(2,128)}, u32[]{:S(2)}) copy-start(f32[1,2,4,128]{3,1,2,0:T(2,128)} %copy-done.19) | copy-start | bytes 12292
  512.7 9.4 %copy-start.24 = (f32[768]{0:T(1024)S(1)}, f32[768]{0:T(1024)}, u32[]{:S(2)}) copy-start(f32[768]{0:T(1024)} %copy-done.23) | copy-start | bytes 9220
  512.7 107.7 %collective-permute-start.4 = (bf16[1536,768]{1,0:T(8,128)(2,1)}, bf16[1536,768]{1,0:T(8,128)(2,1)}, u32[]{:S(2)}, u32[]{:S(2)}) collective-permute-start(bf16[1536,768]{1,0:T(8,128)(2,1)} %maximum_select_fusion.2), channel_id=1, source_target_pairs={{0,16},{1,17},{2,18},{3,19},{4,20},{5,21},{6,22},{7,23},{8,24},{9,... | collective-permute-start | bytes 7077896 | tf_op jit(solution)/shard_map/ppermute | solution.py:67
  522.1 10.6 %copy-start.30 = (f32[1,2,4,128]{3,1,2,0:T(2,128)S(1)}, f32[1,2,4,128]{3,1,2,0:T(2,128)}, u32[]{:S(2)}) copy-start(f32[1,2,4,128]{3,1,2,0:T(2,128)} %copy-done.29) | copy-start | bytes 12292
  522.1 10.6 %copy-start.22 = (f32[1024]{0:T(1024)S(1)}, f32[1024]{0:T(1024)}, u32[]{:S(2)}) copy-start(f32[1024]{0:T(1024)} %copy-done.21) | copy-start | bytes 12292
  531.3 89.1 %copy-start.33 = (f32[768]{0:T(1024)S(1)}, f32[768]{0:T(1024)}, u32[]{:S(2)}) copy-start(f32[768]{0:T(1024)} %copy-done.32) | copy-start | bytes 9220
  (4 other events, 4.5 us)
Sparse Core Ops, SparseCore 0:
  11.0 62.8 all-gather.4
  76.9 52.7 all-gather.6
  132.6 62.4 all-gather.8
  197.9 61.8 all-gather.10
  292.9 23.8 reduce-scatter.12
  363.2 38.8 reduce-scatter.8
  404.6 47.9 reduce-scatter.16
  455.1 47.9 reduce-scatter.20
  507.0 146.5 reduce-scatter.14
  657.4 65.6 reduce-scatter.10
  727.2 68.4 reduce-scatter.18
  799.6 68.9 reduce-scatter.22
